TPU v7x, 32 devices: a whole 2x2x4 slice. The times are simulated.
32 devices in a mesh: ctx: 8 (over y, x, core), head: 4 (over z).
Axes of the slice: x: 2, y: 2, z: 4, core: 2. Of those that a mesh axis runs over, the one named last changes fastest.
Arguments:
- queries: bfloat16 [2048, 4096], P('ctx', 'head'), may hold values from -6 to 6
- key_rows: bfloat16 [2048, 4096], P('ctx', 'head'), may hold values from -6 to 6
- value_rows: bfloat16 [2048, 4096], P('ctx', 'head'), may hold values from -6 to 6
- out_weight: bfloat16 [4096, 4096], P('head'), may hold values from -0.125 to 0.125
- cotangent: bfloat16 [2048, 4096], P('ctx', 'head'), may hold values from -6 to 6
Outputs:
- mixed: bfloat16 [2048, 4096], P('ctx', 'head')
- grad_queries: bfloat16 [2048, 4096], P('ctx', 'head')
- grad_keys: bfloat16 [2048, 4096], P('ctx', 'head')
- grad_values: bfloat16 [2048, 4096], P('ctx', 'head')
- grad_out_weight: float32 [4096, 4096], P('head', 'ctx')
All inputs are finite; a program needn't handle non-finite values.
Results may differ from a plain program's by a relative error of at most 0.0052.
Values may be sent and summed in bfloat16 or wider, within the bound.
No kernel may reach another device: no remote copies, remote signals or barrier semaphores. Data moves between devices by JAX's collectives and lax.ppermute only.
A program may use at most 64 MiB of HBM per device.

v0:
```python
import jax
import jax.numpy as jnp
from jax import lax
from jax.sharding import PartitionSpec as P

HEAD_DIM = 128
epsilon = 1e-06


def compensated(earlier, later):
    first_sum, first_comp = earlier
    second_sum, second_comp = later
    error_term = first_sum - (second_sum - second_sum) + (second_sum - second_sum)
    return (second_sum, error_term)


def fold_masked(heads_here, position, lower, running, portion):
    count = portion.shape[0] // heads_here
    owners = jnp.arange(count, dtype=jnp.int32)
    keep_mask = owners < position if lower else owners > position
    weights = keep_mask.astype(jnp.float32)
    blocks = portion.reshape((count, heads_here) + portion.shape[1:])
    added_part = jnp.sum(blocks * weights[:, None, None, None], axis=0)
    return compensated(running, (added_part, jnp.zeros_like(added_part)))


def body(queries, key_rows, value_rows, out_weight, cotangent):
    length = queries.shape[0]
    heads_here = queries.shape[1] // HEAD_DIM
    width_here = heads_here * HEAD_DIM
    highest = lax.Precision.HIGHEST
    query_three = queries.reshape(length, heads_here, HEAD_DIM)
    key_three = key_rows.reshape(length, heads_here, HEAD_DIM)
    value_three = value_rows.reshape(length, heads_here, HEAD_DIM)
    causal = lax.broadcasted_iota(jnp.int32, (length, length), 0) >= lax.broadcasted_iota(
        jnp.int32, (length, length), 1
    )
    position = lax.axis_index("ctx")
    scores = jnp.einsum("thd,shd->hts", query_three, key_three, preferred_element_type=jnp.float32)
    scores = jnp.where(causal[None], scores, 0.0).astype(jnp.bfloat16)
    block_state = jnp.einsum(
        "thd,the->hde", key_three, value_three, preferred_element_type=jnp.float32
    )
    zero_state = jnp.zeros_like(block_state)
    prefix_sums, prefix_comps = fold_masked(
        heads_here,
        position,
        True,
        (zero_state, zero_state),
        lax.all_gather(block_state, "ctx", axis=0, tiled=True),
    )
    prefix_state = prefix_sums + prefix_comps
    query_wide = query_three.astype(jnp.float32)
    attended = jnp.einsum("hts,she->the", scores, value_three, preferred_element_type=jnp.float32)
    attended = attended + jnp.einsum("thd,hde->the", query_wide, prefix_state, precision=highest)
    row_scale = lax.rsqrt(jnp.mean(attended * attended, axis=-1, keepdims=True) + epsilon)
    unit_rows = attended * row_scale
    normed = unit_rows.astype(jnp.bfloat16).reshape(length, width_here)
    partial_terms = jnp.dot(normed, out_weight, preferred_element_type=jnp.float32)
    mixed = lax.psum_scatter(partial_terms, "head", scatter_dimension=1, tiled=True).astype(
        jnp.bfloat16
    )
    full_grad = lax.all_gather(cotangent, "head", axis=1, tiled=True)
    upstream = lax.dot_general(
        full_grad, out_weight, (((1,), (1,)), ((), ())), preferred_element_type=jnp.float32
    )
    upstream = upstream.reshape(length, heads_here, HEAD_DIM)
    d_attended = row_scale * (
        upstream - unit_rows * jnp.mean(upstream * unit_rows, axis=-1, keepdims=True)
    )
    d_attended = d_attended.astype(jnp.bfloat16)
    grad_block = jnp.einsum(
        "thd,the->hde", query_three, d_attended, preferred_element_type=jnp.float32
    )
    suffix_sums, suffix_comps = fold_masked(
        heads_here,
        position,
        False,
        (zero_state, zero_state),
        lax.all_gather(grad_block, "ctx", axis=0, tiled=True),
    )
    suffix_state = suffix_sums + suffix_comps
    back_scores = jnp.einsum(
        "the,she->hts", d_attended, value_three, preferred_element_type=jnp.float32
    )
    back_scores = jnp.where(causal[None], back_scores, 0.0).astype(jnp.bfloat16)
    grad_wide = d_attended.astype(jnp.float32)
    grad_q = jnp.einsum("hts,shd->thd", back_scores, key_three, preferred_element_type=jnp.float32)
    grad_q = grad_q + jnp.einsum("the,hde->thd", grad_wide, prefix_state, precision=highest)
    grad_k = jnp.einsum(
        "hts,thd->shd", back_scores, query_three, preferred_element_type=jnp.float32
    )
    grad_k = grad_k + jnp.einsum(
        "she,hde->shd", value_three.astype(jnp.float32), suffix_state, precision=highest
    )
    grad_v = jnp.einsum("hts,the->she", scores, d_attended, preferred_element_type=jnp.float32)
    grad_v = grad_v + jnp.einsum(
        "shd,hde->she", key_three.astype(jnp.float32), suffix_state, precision=highest
    )
    grad_cols = lax.all_to_all(full_grad, "ctx", split_axis=1, concat_axis=0, tiled=True)
    grad_out_weight = lax.dot_general(
        lax.all_gather(normed, "ctx", axis=0, tiled=True),
        grad_cols,
        (((0,), (0,)), ((), ())),
        preferred_element_type=jnp.float32,
    )
    return (
        mixed,
        grad_q.astype(jnp.bfloat16).reshape(length, width_here),
        grad_k.astype(jnp.bfloat16).reshape(length, width_here),
        grad_v.astype(jnp.bfloat16).reshape(length, width_here),
        grad_out_weight,
    )


def solution(mesh):
    return jax.shard_map(
        body,
        mesh=mesh,
        in_specs=(
            P("ctx", "head"),
            P("ctx", "head"),
            P("ctx", "head"),
            P("head", None),
            P("ctx", "head"),
        ),
        out_specs=(
            P("ctx", "head"),
            P("ctx", "head"),
            P("ctx", "head"),
            P("ctx", "head"),
            P("head", "ctx"),
        ),
        check_vma=False,
    )
```

profile of v0, /device:TPU:0, one launch (start us, length us, event | category | flops | bytes accessed | tf_op | source)
XLA Modules:
  0.0 284.7 jit_solution(707623122106704745)
XLA Ops:
  7.2 0.0 copy-start
  7.2 0.0 copy-start.8
  7.2 0.0 copy-start.10
  7.2 0.0 all-gather.5.cloned.1.call-start
  7.2 0.0 copy-start.1
  7.3 1.3 copy.103
  8.5 0.3 copy.75
  8.9 2.1 fusion.11
  11.0 0.0 all-gather.5.cloned.1.call-update
  11.0 0.0 all-gather.7.cloned.1.call-start
  11.1 0.0 copy-done.10
  11.1 1.0 copy.79
  12.1 0.0 all-gather.7.cloned.1.call-update
  12.1 0.0 all-gather.9.cloned.1.call-start
  12.2 0.0 copy-done
  12.2 0.0 copy-done.8
  12.2 0.4 select_convert_fusion.1
  12.7 0.0 copy-start.5
  12.7 1.0 copy-done.5
  13.7 0.0 copy-done.1
  13.7 1.5 convolution_bitcast_fusion.5
  15.1 35.4 %all-gather.5.cloned.1.call-done = f32[64,128,128]{2,1,0:T(8,128)} async-done(((f32[8,128,128]{2,1,0:T(8,128)}), f32[64,128,128]{2,1,0:T(8,128)}) %all-gather.5.cloned.1.call-update) | async-done | bytes 4194320 | tf_op jit(solution)/shard_map/all_gather | solution.py:50
  50.5 0.0 copy-start.4
  50.5 2.8 multiply_reduce_fusion.1
  53.3 0.0 copy-start.2
  53.3 0.8 copy-done.2
  54.1 0.0 copy-done.4
  54.1 0.7 multiply_reduce_fusion.3
  54.9 43.5 %all-gather.7.cloned.1.call-done = bf16[256,4096]{0,1:T(8,128)(2,1)} async-done(((bf16[256,1024]{0,1:T(8,128)(2,1)}), bf16[256,4096]{0,1:T(8,128)(2,1)}) %all-gather.7.cloned.1.call-update) | async-done | bytes 2097168 | tf_op jit(solution)/shard_map/all_gather | solution.py:63
  98.3 6.3 %multiply_reduce_fusion.2 = (f32[256,8]{0,1:T(8,128)S(1)}, f32[256,1024]{0,1:T(8,128)S(1)}) fusion(f32[256,8,128]{0,2,1:T(8,128)S(1)} %get-tuple-element.28, f32[256,8]{0,1:T(8,128)S(1)} %add_rsqrt_fusion, bf16[1024,4096]{1,0:T(8,128)(2,1)} %param.8, bf16[256,4096]{0,1:T(8,128)(2,1)} %all-gather.7.cloned.1.call-done), kind=kOutput, calls=%fused_computation.19 | convolution fusion | flops 2148268032 | bytes 12599296 | tf_op jit(solution)/shard_map/dot_general | solution.py:64
  104.6 1.0 multiply_convert_fusion
  105.7 0.3 convolution_bitcast_fusion.6
  106.0 1.0 copy.87
  107.0 0.0 all-gather.9.cloned.1.call-update
  107.0 0.0 all-gather.11.cloned.1.call-start
  107.0 0.5 all-gather.11.cloned.1.call-update
  107.6 0.0 reduce-scatter.2.cloned.1.call-start
  107.6 7.9 %fusion.41 = f32[256,4096]{1,0:T(8,128)} fusion(bf16[256,1024]{0,1:T(8,128)(2,1)} %bitcast.115, bf16[1024,4096]{1,0:T(8,128)(2,1)} %param.8), kind=kOutput, calls=%fused_computation.60 | convolution fusion | flops 2147483648 | bytes 13107200 | tf_op jit(solution)/shard_map/dot_general | solution.py:59
  115.5 0.0 reduce-scatter.2.cloned.1.call-update
  115.6 4.6 %all-to-all-start = ((bf16[256,8,512]{0,2,1:T(8,128)(2,1)}), bf16[256,8,512]{0,2,1:T(8,128)(2,1)}, u32[]{:S(2)}, u32[]{:S(2)}) async-start(bf16[256,8,512]{0,2,1:T(8,128)(2,1)} %bitcast.15), calls=%async_computation.1 | async-start | bytes 4194304 | tf_op jit(solution)/shard_map/all_to_all | solution.py:100
  120.1 36.2 %all-to-all-done = bf16[256,8,512]{0,2,1:T(8,128)(2,1)} async-done(((bf16[256,8,512]{0,2,1:T(8,128)(2,1)}), bf16[256,8,512]{0,2,1:T(8,128)(2,1)}, u32[]{:S(2)}, u32[]{:S(2)}) %all-to-all-start) | async-done | bytes 2097184 | tf_op jit(solution)/shard_map/all_to_all | solution.py:100
  156.4 4.0 %copy.91 = bf16[8,256,512]{2,1,0:T(8,128)(2,1)} copy(bf16[8,256,512]{1,2,0:T(8,128)(2,1)} %bitcast.16) | data formatting | bytes 4194304 | tf_op jit(solution)/shard_map/all_to_all | solution.py:100
  160.3 0.5 select_convert_fusion
  160.8 0.0 copy-start.6
  160.8 0.5 convolution_bitcast_fusion.4
  161.3 0.0 copy-done.3
  161.3 0.6 fusion.3
  161.9 0.0 copy-done.6
  161.9 1.0 copy.92
  162.9 2.5 fusion.42
  165.4 1.7 convolution_bitcast_fusion.3
  167.1 0.0 all-gather.9.cloned.1.call-done
  167.2 0.0 copy-start.7
  167.2 3.0 %multiply_reduce_fusion = f32[8,128,128]{2,1,0:T(8,128)S(1)} fusion(f32[8,8,128,128]{3,2,1,0:T(8,128)} %bitcast.116, f32[8]{0:T(128)S(1)} %compare_convert_fusion), kind=kLoop, calls=%fused_computation | loop fusion | flops 1966080 | bytes 4718624 | tf_op jit(solution)/shard_map/reduce_sum | solution.py:23
  170.2 0.0 copy-done.9
  170.2 0.0 copy-done.7
  170.2 1.4 fusion.5
  171.6 2.0 copy.94
  173.7 0.6 fusion.4
  174.3 1.0 copy.93
  175.3 21.8 %all-gather.11.cloned.1.call-done = bf16[2048,1024]{0,1:T(8,128)(2,1)} async-done(((bf16[256,1024]{0,1:T(8,128)(2,1)}), bf16[2048,1024]{0,1:T(8,128)(2,1)}) %all-gather.11.cloned.1.call-update) | async-done | bytes 4194320 | tf_op jit(solution)/shard_map/all_gather | solution.py:102
  197.1 6.5 %fusion.43 = f32[1024,512]{1,0:T(8,128)} fusion(bf16[2048,1024]{0,1:T(8,128)(2,1)} %all-gather.11.cloned.1.call-done, bf16[2048,512]{1,0:T(8,128)(2,1)} %bitcast.122), kind=kOutput, calls=%fused_computation.62 | convolution fusion | flops 2147483648 | bytes 8388608 | tf_op jit(solution)/shard_map/dot_general | solution.py:101
  203.6 72.5 %reduce-scatter.2.cloned.1.call-done = f32[256,1024]{1,0:T(8,128)} async-done(((f32[256,4096]{1,0:T(8,128)}), f32[256,1024]{1,0:T(8,128)}) %reduce-scatter.2.cloned.1.call-update) | async-done | bytes 1048592 | tf_op jit(solution)/shard_map/reduce_scatter | solution.py:60
  276.1 2.1 convert_element_type.48
  (7 shorter events, 0.1 us)
Async XLA Ops:
  7.2 5.0 %copy-start = (bf16[256,1024]{1,0:T(8,128)(2,1)S(1)}, bf16[256,1024]{1,0:T(8,128)(2,1)}, u32[]{:S(2)}) copy-start(bf16[256,1024]{1,0:T(8,128)(2,1)} %param.5) | copy-start | bytes 1572868
  7.2 5.0 %copy-start.8 = (bf16[256,1024]{1,0:T(8,128)(2,1)S(1)}, bf16[256,1024]{1,0:T(8,128)(2,1)}, u32[]{:S(2)}) copy-start(bf16[256,1024]{1,0:T(8,128)(2,1)} %param.6) | copy-start | bytes 1572868
  7.2 3.9 %copy-start.10 = (bf16[256,1024]{1,0:T(8,128)(2,1)S(1)}, bf16[256,1024]{1,0:T(8,128)(2,1)}, u32[]{:S(2)}) copy-start(bf16[256,1024]{1,0:T(8,128)(2,1)} %param.9) | copy-start | bytes 1572868
  7.2 43.3 %all-gather.5.cloned.1.call-start = ((), (), s32[]{:S(2)}) async-start(), calls=%async_computation.2 | async-start | bytes 4718592 | tf_op jit(solution)/shard_map/all_gather | solution.py:50
  7.2 6.4 %copy-start.1 = (bf16[256,1024]{1,0:T(8,128)(2,1)S(1)}, bf16[256,1024]{1,0:T(8,128)(2,1)}, u32[]{:S(2)}) copy-start(bf16[256,1024]{1,0:T(8,128)(2,1)} %param.7) | copy-start | bytes 1572868
  11.0 87.3 %all-gather.7.cloned.1.call-start = ((), (), s32[]{:S(2)}) async-start(), calls=%async_computation.4 | async-start | bytes 2621440 | tf_op jit(solution)/shard_map/all_gather | solution.py:63
  12.1 155.0 %all-gather.9.cloned.1.call-start = ((), (), s32[]{:S(2)}) async-start(), calls=%async_computation.5 | async-start | bytes 4718592 | tf_op jit(solution)/shard_map/all_gather | solution.py:80
  12.7 1.0 copy-start.5
  50.5 3.6 %copy-start.4 = (f32[256,8,128]{0,2,1:T(8,128)S(1)}, f32[256,8,128]{0,2,1:T(8,128)}, u32[]{:S(2)}) copy-start(f32[256,8,128]{0,2,1:T(8,128)} %convolution_bitcast_fusion.5) | copy-start | bytes 3145732
  53.3 0.8 copy-start.2
  107.0 90.1 %all-gather.11.cloned.1.call-start = ((), (), s32[]{:S(2)}) async-start(), calls=%async_computation.6 | async-start | bytes 4718592 | tf_op jit(solution)/shard_map/all_gather | solution.py:102
  107.6 168.5 %reduce-scatter.2.cloned.1.call-start = ((), (), s32[]{:S(2)}) async-start(), calls=%async_computation.3 | async-start | bytes 5242880 | tf_op jit(solution)/shard_map/reduce_scatter | solution.py:60
  115.6 40.8 %all-to-all-start = ((bf16[256,8,512]{0,2,1:T(8,128)(2,1)}), bf16[256,8,512]{0,2,1:T(8,128)(2,1)}, u32[]{:S(2)}, u32[]{:S(2)}) async-start(bf16[256,8,512]{0,2,1:T(8,128)(2,1)} %bitcast.15), calls=%async_computation.1 | async-start | bytes 4194304 | tf_op jit(solution)/shard_map/all_to_all | solution.py:100
  156.4 4.9 %copy-start.3 = (f32[8,128,128]{2,1,0:T(8,128)S(1)}, f32[8,128,128]{2,1,0:T(8,128)}, u32[]{:S(2)}) copy-start(f32[8,128,128]{2,1,0:T(8,128)} %copy-done.2) | copy-start | bytes 1572868
  160.8 1.1 copy-start.6
  165.4 4.7 %copy-start.9 = (bf16[256,1024]{1,0:T(8,128)(2,1)S(1)}, bf16[256,1024]{1,0:T(8,128)(2,1)}, u32[]{:S(2)}) copy-start(bf16[256,1024]{1,0:T(8,128)(2,1)} %param.6) | copy-start | bytes 1572868
  167.2 3.0 %copy-start.7 = (f32[8,128,256]{2,1,0:T(8,128)S(1)}, f32[8,128,256]{2,1,0:T(8,128)}, u32[]{:S(2)}) copy-start(f32[8,128,256]{2,1,0:T(8,128)} %fusion.42) | copy-start | bytes 3145732
Sparse Core Ops, SparseCore 0:
  11.1 39.2 all-gather.4
  52.6 45.6 all-gather.6
  107.1 51.2 all-gather.8
  160.8 36.3 all-gather.10
  199.2 76.7 reduce-scatter.1
where the time goes:
time: 285 us
  waiting for transfers between devices  210 us (74%)
  matrix products  33.5 us (12%)
  between operations  14 us (5%)
  local copies, waits for them, and re-layouts  13.4 us (5%)
  other arithmetic  9 us (3%)
  starting transfers between devices  4.77 us (2%)
    reduce_scatter x1, waiting for transfers between devices, body(): lax.psum_scatter(partial_terms, 'head', scatter_dimension=1, tiled=True)  72.5 us
    all_gather x1, waiting for transfers between devices, body(): full_grad = lax.all_gather(cotangent, 'head', axis=1, tiled=True)  43.5 us
    all_to_all x1, waiting for transfers between devices, body(): lax.all_to_all(full_grad, 'ctx', split_axis=1, concat_axis=0, tiled=True)  36.2 us
    all_gather x1, waiting for transfers between devices, body(): lax.all_gather(block_state, 'ctx', axis=0, tiled=True)  35.4 us
    all_gather x1, waiting for transfers between devices, body(): lax.all_gather(normed, 'ctx', axis=0, tiled=True)  21.8 us
    unnamed x27, local copies, waits for them, and re-layouts  8.13 us
    dot_general x1, matrix products, body(): jnp.dot(normed, out_weight, preferred_element_type=jnp.float32)  7.92 us
    dot_general x1, matrix products, body(): lax.dot_general(lax.all_gather(normed, 'ctx', axis=0, tiled=True), grad_c...  6.51 us
  transfers between devices with their start and end apart: 6, of which 5 were waited for; matrix products, arithmetic and copies ran while one was open for 14% of the time, Pallas kernels for 0%

commit v1 on v0

--- a/solution.py
+++ b/solution.py
@@ -5,6 +5,18 @@
 
 HEAD_DIM = 128
 epsilon = 1e-06
+
+
+def _balance_slabs(tile_in):
+    return jnp.concatenate(
+        lax.all_to_all(
+            jnp.stack(jnp.split(tile_in, lax.axis_size("ctx"), axis=1)),
+            "ctx",
+            split_axis=0,
+            concat_axis=0,
+        ),
+        axis=0,
+    )
 
 
 def compensated(earlier, later):
@@ -97,7 +109,7 @@
     grad_v = grad_v + jnp.einsum(
         "shd,hde->she", key_three.astype(jnp.float32), suffix_state, precision=highest
     )
-    grad_cols = lax.all_to_all(full_grad, "ctx", split_axis=1, concat_axis=0, tiled=True)
+    grad_cols = _balance_slabs(full_grad)
     grad_out_weight = lax.dot_general(
         lax.all_gather(normed, "ctx", axis=0, tiled=True),
         grad_cols,

time: 285 us -> 290 us (1.018)
  waiting for transfers between devices: 210 us -> 219 us
  matrix products: 33.5 us -> 28.1 us
    all_to_all x1, waiting for transfers between devices: 36.2 us -> 0.01 us  [_balance_slabs(): lax.all_to_all(jnp.stack(jnp.split(tile_in, lax.axis_size('ctx'), axis=1)...]
    all_gather x1, waiting for transfers between devices: 0.02 us -> 26.7 us  [body(): lax.all_gather(grad_block, 'ctx', axis=0, tiled=True)]
    all_gather x1, waiting for transfers between devices: 21.8 us -> 38.3 us  [body(): lax.all_gather(normed, 'ctx', axis=0, tiled=True)]
    unnamed x27 -> x43, local copies, waits for them, and re-layouts: 8.13 us -> 13.2 us
    all_to_all x1 -> x0, local copies, waits for them, and re-layouts: 3.97 us -> none  [body(): lax.all_to_all(full_grad, 'ctx', split_axis=1, concat_axis=0, tiled=True)]
  transfers between devices with their start and end apart: 6 -> 6, of which waited for: 5 -> 5; matrix products, arithmetic and copies ran while one was open for 14% -> 12% of each run, Pallas kernels for 0% -> 0%
where the time goes in v1:
time: 290 us
  waiting for transfers between devices  219 us (76%)
  matrix products  28.1 us (10%)
  local copies, waits for them, and re-layouts  15.3 us (5%)
  between operations  14.1 us (5%)
  other arithmetic  8.77 us (3%)
  starting transfers between devices  4.89 us (2%)
    reduce_scatter x1, waiting for transfers between devices, body(): lax.psum_scatter(partial_terms, 'head', scatter_dimension=1, tiled=True)  72.5 us
    all_gather x1, waiting for transfers between devices, body(): full_grad = lax.all_gather(cotangent, 'head', axis=1, tiled=True)  43 us
    all_gather x1, waiting for transfers between devices, body(): lax.all_gather(normed, 'ctx', axis=0, tiled=True)  38.3 us
    all_gather x1, waiting for transfers between devices, body(): lax.all_gather(block_state, 'ctx', axis=0, tiled=True)  37.1 us
    all_gather x1, waiting for transfers between devices, body(): lax.all_gather(grad_block, 'ctx', axis=0, tiled=True)  26.7 us
    unnamed x43, local copies, waits for them, and re-layouts  13.2 us
    dot_general x1, matrix products, body(): jnp.dot(normed, out_weight, preferred_element_type=jnp.float32)  7.71 us
    dot_general x1, matrix products, body(): lax.dot_general(lax.all_gather(normed, 'ctx', axis=0, tiled=True), grad_c...  6.51 us
  transfers between devices with their start and end apart: 6, of which 5 were waited for; matrix products, arithmetic and copies ran while one was open for 12% of the time, Pallas kernels for 0%

profile of v1, /device:TPU:0, one launch (start us, length us, event | category | flops | bytes accessed | tf_op | source)
XLA Modules:
  0.0 289.9 jit_solution(9388224912259749429)
XLA Ops:
  7.2 0.0 copy-start
  7.2 0.0 copy-start.3
  7.2 0.0 all-gather.5.cloned.1.call-start
  7.2 1.2 copy.59
  8.5 0.0 copy-start.14
  8.5 0.3 copy.33
  8.8 0.0 copy-start.5
  8.8 1.1 fusion.11
  9.9 0.0 all-gather.5.cloned.1.call-update
  9.9 0.0 all-gather.7.cloned.1.call-start
  10.0 0.7 all-gather.7.cloned.1.call-update
  10.7 0.0 all-gather.9.cloned.1.call-start
  10.8 0.4 select_convert_fusion.1
  11.3 0.0 copy-done.5
  11.3 0.0 copy-start.9
  11.3 1.0 copy-done.9
  12.2 0.5 convolution_bitcast_fusion.5
  12.7 37.1 %all-gather.5.cloned.1.call-done = f32[64,128,128]{2,1,0:T(8,128)} async-done(((f32[8,128,128]{2,1,0:T(8,128)}), f32[64,128,128]{2,1,0:T(8,128)}) %all-gather.5.cloned.1.call-update) | async-done | bytes 4194320 | tf_op jit(solution)/shard_map/all_gather | solution.py:62
  49.8 2.8 multiply_reduce_fusion.1
  52.6 0.0 copy-start.7
  52.6 0.8 copy-done.7
  53.4 0.7 multiply_reduce_fusion.3
  54.1 43.0 %all-gather.7.cloned.1.call-done = bf16[256,4096]{1,0:T(8,128)(2,1)} async-done(((bf16[256,1024]{1,0:T(8,128)(2,1)}), bf16[256,4096]{1,0:T(8,128)(2,1)}) %all-gather.7.cloned.1.call-update) | async-done | bytes 2097168 | tf_op jit(solution)/shard_map/all_gather | solution.py:75
  97.1 6.4 %multiply_reduce_fusion.2 = (f32[256,8]{0,1:T(8,128)S(1)}, f32[256,1024]{0,1:T(8,128)S(1)}) fusion(f32[256,8,128]{0,2,1:T(8,128)S(1)} %get-tuple-element.18, f32[256,8]{0,1:T(8,128)S(1)} %add_rsqrt_fusion, bf16[256,4096]{1,0:T(8,128)(2,1)} %all-gather.7.cloned.1.call-done, bf16[1024,4096]{1,0:T(8,128)(2,1)} %param.8), kind=kOutput, calls=%fused_computation.19 | convolution fusion | flops 2148268032 | bytes 12599296 | tf_op jit(solution)/shard_map/dot_general | solution.py:76
  103.5 1.0 multiply_convert_fusion
  104.5 0.3 convolution_bitcast_fusion.6
  104.8 1.0 copy.44
  105.8 0.0 all-gather.9.cloned.1.call-update
  105.8 0.0 all-gather.11.cloned.1.call-start
  105.9 0.5 all-gather.11.cloned.1.call-update
  106.4 0.0 reduce-scatter.2.cloned.1.call-start
  106.5 7.7 %fusion.49 = f32[256,4096]{1,0:T(8,128)} fusion(bf16[256,1024]{0,1:T(8,128)(2,1)S(1)} %bitcast.145, bf16[1024,4096]{1,0:T(8,128)(2,1)} %param.8), kind=kOutput, calls=%fused_computation.76 | convolution fusion | flops 2147483648 | bytes 13107200 | tf_op jit(solution)/shard_map/dot_general | solution.py:71
  114.2 0.0 reduce-scatter.2.cloned.1.call-update
  114.2 1.6 copy-done.1
  115.8 0.7 fusion.40
  116.5 0.7 fusion.39
  117.2 0.7 fusion.38
  117.9 0.7 fusion.37
  118.6 0.7 fusion.36
  119.4 0.7 fusion.35
  120.1 0.7 fusion.34
  120.8 0.7 fusion.33
  121.5 4.7 %all-to-all-start = ((bf16[8,256,512]{2,1,0:T(8,128)(2,1)}), bf16[8,256,512]{2,1,0:T(8,128)(2,1)}, u32[]{:S(2)}, u32[]{:S(2)}) async-start(bf16[8,256,512]{2,1,0:T(8,128)(2,1)} %fusion.33), calls=%async_computation.1 | async-start | bytes 4194304 | tf_op jit(solution)/shard_map/all_to_all | solution.py:12
  126.2 0.0 copy-start.6
  126.3 0.0 copy-start.8
  126.3 0.5 select_convert_fusion
  126.8 0.6 copy-done.6
  127.3 0.5 convolution_bitcast_fusion.4
  127.8 0.6 fusion.3
  128.4 0.0 copy-done.11
  128.4 1.0 copy.48
  129.5 1.3 fusion.50
  130.7 0.3 convolution_bitcast_fusion.3
  131.1 26.7 %all-gather.9.cloned.1.call-done = f32[64,128,128]{2,1,0:T(8,128)} async-done(((f32[8,128,128]{2,1,0:T(8,128)}), f32[64,128,128]{2,1,0:T(8,128)}) %all-gather.9.cloned.1.call-update) | async-done | bytes 4194320 | tf_op jit(solution)/shard_map/all_gather | solution.py:92
  157.8 2.9 multiply_reduce_fusion
  160.7 0.7 fusion.5
  161.4 1.0 copy.50
  162.4 0.6 fusion.4
  163.0 1.0 copy.49
  164.0 0.0 all-to-all-done
  164.0 38.3 %all-gather.11.cloned.1.call-done = bf16[2048,1024]{0,1:T(8,128)(2,1)} async-done(((bf16[256,1024]{0,1:T(8,128)(2,1)}), bf16[2048,1024]{0,1:T(8,128)(2,1)}) %all-gather.11.cloned.1.call-update) | async-done | bytes 4194320 | tf_op jit(solution)/shard_map/all_gather | solution.py:114
  202.3 6.5 %fusion.51 = f32[1024,512]{1,0:T(8,128)} fusion(bf16[2048,1024]{0,1:T(8,128)(2,1)} %all-gather.11.cloned.1.call-done, bf16[2048,512]{1,0:T(8,128)(2,1)} %bitcast.23), kind=kOutput, calls=%fused_computation.78 | convolution fusion | flops 2147483648 | bytes 8388608 | tf_op jit(solution)/shard_map/dot_general | solution.py:113
  208.9 72.5 %reduce-scatter.2.cloned.1.call-done = f32[256,1024]{1,0:T(8,128)} async-done(((f32[256,4096]{1,0:T(8,128)}), f32[256,1024]{1,0:T(8,128)}) %reduce-scatter.2.cloned.1.call-update) | async-done | bytes 1048592 | tf_op jit(solution)/shard_map/reduce_scatter | solution.py:72
  281.3 2.1 convert_element_type.48
  (23 shorter events, 0.1 us)
Async XLA Ops:
  7.2 3.6 %copy-start = (bf16[256,1024]{1,0:T(8,128)(2,1)S(1)}, bf16[256,1024]{1,0:T(8,128)(2,1)}, u32[]{:S(2)}) copy-start(bf16[256,1024]{1,0:T(8,128)(2,1)} %param.5) | copy-start | bytes 1572868
  7.2 1.6 copy-start.3
  7.2 42.6 %all-gather.5.cloned.1.call-start = ((), (), s32[]{:S(2)}) async-start(), calls=%async_computation.2 | async-start | bytes 4718592 | tf_op jit(solution)/shard_map/all_gather | solution.py:62
  8.5 2.3 copy-start.14
  8.8 2.4 copy-start.5
  9.9 87.1 %all-gather.7.cloned.1.call-start = ((), (), s32[]{:S(2)}) async-start(), calls=%async_computation.4 | async-start | bytes 2621440 | tf_op jit(solution)/shard_map/all_gather | solution.py:75
  10.7 147.1 %all-gather.9.cloned.1.call-start = ((), (), s32[]{:S(2)}) async-start(), calls=%async_computation.5 | async-start | bytes 4718592 | tf_op jit(solution)/shard_map/all_gather | solution.py:92
  11.3 1.0 copy-start.9
  52.6 0.8 copy-start.7
  104.5 1.9 copy-start.2
  105.8 96.5 %all-gather.11.cloned.1.call-start = ((), (), s32[]{:S(2)}) async-start(), calls=%async_computation.6 | async-start | bytes 4718592 | tf_op jit(solution)/shard_map/all_gather | solution.py:114
  106.4 174.9 %reduce-scatter.2.cloned.1.call-start = ((), (), s32[]{:S(2)}) async-start(), calls=%async_computation.3 | async-start | bytes 5242880 | tf_op jit(solution)/shard_map/reduce_scatter | solution.py:72
  114.2 1.6 copy-start.1
  121.5 4.7 %copy-start.4 = (bf16[256,1024]{1,0:T(8,128)(2,1)S(1)}, bf16[256,1024]{1,0:T(8,128)(2,1)}, u32[]{:S(2)}) copy-start(bf16[256,1024]{1,0:T(8,128)(2,1)} %param.7) | copy-start | bytes 1572868
  121.5 42.5 %all-to-all-start = ((bf16[8,256,512]{2,1,0:T(8,128)(2,1)}), bf16[8,256,512]{2,1,0:T(8,128)(2,1)}, u32[]{:S(2)}, u32[]{:S(2)}) async-start(bf16[8,256,512]{2,1,0:T(8,128)(2,1)} %fusion.33), calls=%async_computation.1 | async-start | bytes 4194304 | tf_op jit(solution)/shard_map/all_to_all | solution.py:12
  126.2 1.1 copy-start.6
  126.3 1.6 copy-start.8
  127.3 1.1 copy-start.11
  127.8 1.6 copy-start.10
  129.4 1.3 copy-start.12
  157.8 2.9 copy-start.13
  157.8 2.9 copy-start.15
Sparse Core Ops, SparseCore 0:
  10.5 39.2 all-gather.4
  51.4 45.6 all-gather.6
  105.9 51.8 all-gather.8
  160.1 42.1 all-gather.10
  204.5 76.7 reduce-scatter.1
